TPU v7x, 512 devices: a whole 4x4x16 slice. The times are simulated.
512 devices in a mesh: blk: 512 (over x, z, y, core).
Axes of the slice: x: 4, y: 4, z: 16, core: 2. Of those that a mesh axis runs over, the one named last changes fastest.
Arguments:
- rhs: float32 [524288, 256], P('blk'), may hold values from -6 to 6
- diag_inv: float32 [524288, 128], P('blk')
- factor_blocks: float32 [15360, 128, 128], P('blk'), may hold values from -0.125 to 0.125
- order: int32 [4096], P('blk'), may hold values from 0 to 7, as said below
- blk_row: int32 [15360], P('blk'), may hold values from 0 to 4095, as said below
- blk_col: int32 [15360], P('blk'), may hold values from 0 to 4095, as said below
Outputs:
- solution: float32 [524288, 256], P('blk')
Inputs may be any that keep to these rules, and one draw needn't show every extreme that they name: `order`: for each device d, entries d * 8 to d * 8 + 7 are a permutation of 0 to 7. `blk_row`: stored block j lies on device j // 30; with p = j % 30 and k = p // 10, its row is a block row of that same device whose level is above k. `blk_col`: with j, p and k as for blk_row and e = (p // 2) % 5, the 2 blocks that share j // 30, k and e have as columns, each once, the 2 block rows of level k of the device e places below j // 30, counted cyclically over all devices.
All inputs are finite; a program needn't handle non-finite values.
Results may differ from a plain program's by a relative error of at most 0.0001.
Values sent between devices are 32-bit elements; how exact they have to be, the bound alone decides.
No kernel may reach another device: no remote copies, remote signals or barrier semaphores. Data moves between devices by JAX's collectives and lax.ppermute only.
A program may use at most 64 MiB of HBM per device.

v0:
```python
import jax
import jax.numpy as jnp
from jax import lax
from jax.sharding import PartitionSpec as P

LANES = 2
STEPS = 4
BAND = 4


HIGH = lax.Precision.HIGHEST


def from_behind(block, axis, distance):
    devices = range(lax.axis_size(axis))
    route = [((i - distance) % len(devices), i) for i in devices]
    return lax.ppermute(block, axis, route)


def select_rows(picker, stacked):
    return jnp.einsum("ar,rbc->abc", picker, stacked, precision=HIGH)


def body(rhs, diag_inv, factor_blocks, order, blk_row, blk_col):
    slot_count = order.shape[0]
    block_size = diag_inv.shape[1]
    columns = rhs.shape[1]
    lane_count = LANES
    band_reach = BAND
    group_size = (band_reach + 1) * lane_count
    device = lax.axis_index("blk")
    first_row = device * slot_count
    residual = rhs.reshape(slot_count, block_size, columns)
    inverses = diag_inv.reshape(slot_count, block_size, block_size)
    slot_ids = jnp.arange(slot_count, dtype=jnp.int32)
    targets = ((blk_row - first_row)[:, None] == slot_ids[None, :]).astype(jnp.float32)
    solution = jnp.zeros_like(residual)
    shaped_blocks = factor_blocks.reshape(
        STEPS - 1, band_reach + 1, lane_count, block_size, block_size
    )
    shaped_cols = blk_col.reshape(STEPS - 1, band_reach + 1, lane_count)
    for step_index in range(STEPS):
        solving = order[step_index * lane_count : (step_index + 1) * lane_count]
        picker = (solving[:, None] == slot_ids[None, :]).astype(jnp.float32)
        current = select_rows(picker, residual)
        own_inverse = select_rows(picker, inverses)
        solved = jnp.einsum("lij,ljc->lic", own_inverse, current, precision=HIGH)
        solution = solution + jnp.einsum("lr,lbc->rbc", picker, solved, precision=HIGH)
        if step_index + 1 < STEPS:
            labels = first_row + solving
            value_list = [solved]
            label_list = [labels]
            for offset in range(1, band_reach + 1):
                got_values, got_labels = from_behind((solved, labels), "blk", offset)
                value_list.append(got_values)
                label_list.append(got_labels)
            stacked_values = jnp.stack(value_list)
            stacked_labels = jnp.stack(label_list)
            first_block = step_index * group_size
            blocks_now = shaped_blocks[step_index]
            cols_now = shaped_cols[step_index]
            matches = (cols_now[:, :, None] == stacked_labels[:, None, :]).astype(jnp.float32)
            inputs = jnp.einsum("dml,dlbc->dmbc", matches, stacked_values, precision=HIGH)
            product_terms = jnp.einsum("dmij,dmjc->dmic", blocks_now, inputs, precision=HIGH)
            landing = targets[first_block : first_block + group_size].reshape(
                band_reach + 1, lane_count, slot_count
            )
            residual = residual - jnp.einsum(
                "dmr,dmic->ric", landing, product_terms, precision=HIGH
            )
    return solution.reshape(slot_count * block_size, columns)


def solution(mesh):
    placed = (P("blk", None), P("blk", None), P("blk", None, None), P("blk"), P("blk"), P("blk"))
    return jax.shard_map(
        body, mesh=mesh, in_specs=placed, out_specs=P("blk", None), check_vma=False
    )
```

profile of v0, /device:TPU:1, one launch (start us, length us, event | category | flops | bytes accessed | tf_op | source)
XLA Modules:
  0.0 263.5 jit_solution(13338814059749417141)
XLA Ops:
  1.8 2.4 fusion.12
  4.6 4.7 %collective-permute-start.4 = (f32[2,128,256]{2,1,0:T(8,128)S(1)}, f32[2,128,256]{2,1,0:T(8,128)}, u32[]{:S(2)}, u32[]{:S(2)}) collective-permute-start(f32[2,128,256]{2,1,0:T(8,128)S(1)} %get-tuple-element.22), channel_id=1, source_target_pairs={{511,0},{0,1},{1,2},{2,3},{3,4},{4,5},{5,6},{6,7},{7,8},{8,9},{9,1... | collective-permute-start | bytes 786440 | tf_op jit(solution)/shard_map/ppermute | solution.py:17
  9.3 3.2 %collective-permute-start.5 = (f32[2,128,256]{2,1,0:T(8,128)S(1)}, f32[2,128,256]{2,1,0:T(8,128)}, u32[]{:S(2)}, u32[]{:S(2)}) collective-permute-start(f32[2,128,256]{2,1,0:T(8,128)S(1)} %get-tuple-element.22), channel_id=1, source_target_pairs={{510,0},{511,1},{0,2},{1,3},{2,4},{3,5},{4,6},{5,7},{6,8},{7,9},{8... | collective-permute-start | bytes 786440 | tf_op jit(solution)/shard_map/ppermute | solution.py:17
  12.5 3.5 %collective-permute-start.6 = (f32[2,128,256]{2,1,0:T(8,128)S(1)}, f32[2,128,256]{2,1,0:T(8,128)}, u32[]{:S(2)}, u32[]{:S(2)}) collective-permute-start(f32[2,128,256]{2,1,0:T(8,128)S(1)} %get-tuple-element.22), channel_id=1, source_target_pairs={{509,0},{510,1},{511,2},{0,3},{1,4},{2,5},{3,6},{4,7},{5,8},{6,9},... | collective-permute-start | bytes 786440 | tf_op jit(solution)/shard_map/ppermute | solution.py:17
  16.0 3.6 %collective-permute-start.7 = (f32[2,128,256]{2,1,0:T(8,128)S(1)}, f32[2,128,256]{2,1,0:T(8,128)}, u32[]{:S(2)}, u32[]{:S(2)}) collective-permute-start(f32[2,128,256]{2,1,0:T(8,128)S(1)} %get-tuple-element.22), channel_id=1, source_target_pairs={{508,0},{509,1},{510,2},{511,3},{0,4},{1,5},{2,6},{3,7},{4,8},{5,9... | collective-permute-start | bytes 786440 | tf_op jit(solution)/shard_map/ppermute | solution.py:17
  19.7 3.8 %collective-permute-start = (s32[2]{0:T(128)S(1)}, s32[2]{0:T(128)S(1)}, u32[]{:S(2)}, u32[]{:S(2)}) collective-permute-start(s32[2]{0:T(128)S(1)} %get-tuple-element.12), channel_id=1, source_target_pairs={{511,0},{0,1},{1,2},{2,3},{3,4},{4,5},{5,6},{6,7},{7,8},{8,9},{9,1... | collective-permute-start | bytes 32 | tf_op jit(solution)/shard_map/ppermute | solution.py:17
  32.1 2.3 collective-permute-start.1
  34.4 10.5 %collective-permute-done.1 = s32[2]{0:T(128)S(1)} collective-permute-done((s32[2]{0:T(128)S(1)}, s32[2]{0:T(128)S(1)}, u32[]{:S(2)}, u32[]{:S(2)}) %collective-permute-start.1) | collective-permute-done | bytes 40 | tf_op jit(solution)/shard_map/ppermute | solution.py:17
  44.9 1.9 collective-permute-start.2
  46.8 9.7 %collective-permute-done.2 = s32[2]{0:T(128)S(1)} collective-permute-done((s32[2]{0:T(128)S(1)}, s32[2]{0:T(128)S(1)}, u32[]{:S(2)}, u32[]{:S(2)}) %collective-permute-start.2) | collective-permute-done | bytes 40 | tf_op jit(solution)/shard_map/ppermute | solution.py:17
  58.5 8.1 %collective-permute-done.3 = s32[2]{0:T(128)S(1)} collective-permute-done((s32[2]{0:T(128)S(1)}, s32[2]{0:T(128)S(1)}, u32[]{:S(2)}, u32[]{:S(2)}) %collective-permute-start.3) | collective-permute-done | bytes 40 | tf_op jit(solution)/shard_map/ppermute | solution.py:17
  66.6 5.3 %collective-permute-start.8 = (s32[2]{0:T(128)S(1)}, s32[2]{0:T(128)S(1)}, u32[]{:S(2)}, u32[]{:S(2)}) collective-permute-start(s32[2]{0:T(128)S(1)} %get-tuple-element.13), channel_id=1, source_target_pairs={{511,0},{0,1},{1,2},{2,3},{3,4},{4,5},{5,6},{6,7},{7,8},{8,9},{9,1... | collective-permute-start | bytes 32 | tf_op jit(solution)/shard_map/ppermute | solution.py:17
  72.0 6.4 %collective-permute-done.8 = s32[2]{0:T(128)S(1)} collective-permute-done((s32[2]{0:T(128)S(1)}, s32[2]{0:T(128)S(1)}, u32[]{:S(2)}, u32[]{:S(2)}) %collective-permute-start.8) | collective-permute-done | bytes 40 | tf_op jit(solution)/shard_map/ppermute | solution.py:17
  80.3 7.8 %collective-permute-done.9 = s32[2]{0:T(128)S(1)} collective-permute-done((s32[2]{0:T(128)S(1)}, s32[2]{0:T(128)S(1)}, u32[]{:S(2)}, u32[]{:S(2)}) %collective-permute-start.9) | collective-permute-done | bytes 40 | tf_op jit(solution)/shard_map/ppermute | solution.py:17
  90.1 9.5 %collective-permute-done.10 = s32[2]{0:T(128)S(1)} collective-permute-done((s32[2]{0:T(128)S(1)}, s32[2]{0:T(128)S(1)}, u32[]{:S(2)}, u32[]{:S(2)}) %collective-permute-start.10) | collective-permute-done | bytes 40 | tf_op jit(solution)/shard_map/ppermute | solution.py:17
  101.5 8.1 %collective-permute-done.11 = s32[2]{0:T(128)S(1)} collective-permute-done((s32[2]{0:T(128)S(1)}, s32[2]{0:T(128)S(1)}, u32[]{:S(2)}, u32[]{:S(2)}) %collective-permute-start.11) | collective-permute-done | bytes 40 | tf_op jit(solution)/shard_map/ppermute | solution.py:17
  109.6 5.3 %collective-permute-start.16 = (s32[2]{0:T(128)S(1)}, s32[2]{0:T(128)S(1)}, u32[]{:S(2)}, u32[]{:S(2)}) collective-permute-start(s32[2]{0:T(128)S(1)} %get-tuple-element.14), channel_id=1, source_target_pairs={{511,0},{0,1},{1,2},{2,3},{3,4},{4,5},{5,6},{6,7},{7,8},{8,9},{9,1... | collective-permute-start | bytes 32 | tf_op jit(solution)/shard_map/ppermute | solution.py:17
  114.9 6.4 %collective-permute-done.16 = s32[2]{0:T(128)S(1)} collective-permute-done((s32[2]{0:T(128)S(1)}, s32[2]{0:T(128)S(1)}, u32[]{:S(2)}, u32[]{:S(2)}) %collective-permute-start.16) | collective-permute-done | bytes 40 | tf_op jit(solution)/shard_map/ppermute | solution.py:17
  123.3 7.8 %collective-permute-done.17 = s32[2]{0:T(128)S(1)} collective-permute-done((s32[2]{0:T(128)S(1)}, s32[2]{0:T(128)S(1)}, u32[]{:S(2)}, u32[]{:S(2)}) %collective-permute-start.17) | collective-permute-done | bytes 40 | tf_op jit(solution)/shard_map/ppermute | solution.py:17
  133.0 9.5 %collective-permute-done.18 = s32[2]{0:T(128)S(1)} collective-permute-done((s32[2]{0:T(128)S(1)}, s32[2]{0:T(128)S(1)}, u32[]{:S(2)}, u32[]{:S(2)}) %collective-permute-start.18) | collective-permute-done | bytes 40 | tf_op jit(solution)/shard_map/ppermute | solution.py:17
  142.5 2.1 collective-permute-start.19
  144.6 7.9 %collective-permute-done.19 = s32[2]{0:T(128)S(1)} collective-permute-done((s32[2]{0:T(128)S(1)}, s32[2]{0:T(128)S(1)}, u32[]{:S(2)}, u32[]{:S(2)}) %collective-permute-start.19) | collective-permute-done | bytes 40 | tf_op jit(solution)/shard_map/ppermute | solution.py:17
  156.5 3.1 %fusion.7 = f32[5,2,128,256]{3,1,2,0:T(2,128)S(1)} fusion(f32[5,2,128,256]{3,2,1,0:T(8,128)S(1)} %bitcast_dynamic-update-slice_fusion.10, s32[5,2]{1,0:T(8,128)S(1)} %stack.113, s32[5,2]{1,0:T(8,128)S(1)} %eq.119), kind=kOutput, calls=%fused_computation.16 | convolution fusion | flops 7864340 | bytes 2621520 | tf_op jit(solution)/shard_map/dml,dlbc->dmbc/dot_general | solution.py:63
  159.6 2.4 convolution_bitcast_fusion.2
  162.0 2.0 copy.77
  164.0 3.2 %fusion.9 = f32[8,128,256]{2,0,1:T(8,128)S(1)} fusion(f32[5,2,128,256]{3,0,1,2:T(8,128)} %copy.77, f32[8,128,256]{2,1,0:T(8,128)} %bitcast.138, pred[5,2,8]{0,2,1:T(8,128)(4,1)S(1)} %copy.76), kind=kOutput, calls=%fused_computation.18 | convolution fusion | flops 31719424 | bytes 3407952 | tf_op jit(solution)/shard_map/dmr,dmic->ric/dot_general | solution.py:68
  168.6 5.3 %collective-permute-start.12 = (f32[2,128,256]{2,1,0:T(8,128)S(1)}, f32[2,128,256]{2,1,0:T(8,128)S(1)}, u32[]{:S(2)}, u32[]{:S(2)}) collective-permute-start(f32[2,128,256]{2,1,0:T(8,128)S(1)} %get-tuple-element.24), channel_id=1, source_target_pairs={{511,0},{0,1},{1,2},{2,3},{3,4},{4,5},{5,6},{6,7},{7,8},{8,9},{9,1... | collective-permute-start | bytes 786440 | tf_op jit(solution)/shard_map/ppermute | solution.py:17
  173.9 2.8 %collective-permute-start.13 = (f32[2,128,256]{2,1,0:T(8,128)S(1)}, f32[2,128,256]{2,1,0:T(8,128)S(1)}, u32[]{:S(2)}, u32[]{:S(2)}) collective-permute-start(f32[2,128,256]{2,1,0:T(8,128)S(1)} %get-tuple-element.24), channel_id=1, source_target_pairs={{510,0},{511,1},{0,2},{1,3},{2,4},{3,5},{4,6},{5,7},{6,8},{7,9},{8... | collective-permute-start | bytes 786440 | tf_op jit(solution)/shard_map/ppermute | solution.py:17
  176.7 2.3 collective-permute-start.14
  179.0 2.1 collective-permute-start.15
  181.1 2.5 convolution_add_fusion.2
  183.7 15.6 %collective-permute-done.13 = f32[2,128,256]{2,1,0:T(8,128)S(1)} collective-permute-done((f32[2,128,256]{2,1,0:T(8,128)S(1)}, f32[2,128,256]{2,1,0:T(8,128)S(1)}, u32[]{:S(2)}, u32[]{:S(2)}) %collective-permute-start.13) | collective-permute-done | bytes 262176 | tf_op jit(solution)/shard_map/ppermute | solution.py:17
  199.3 6.1 %collective-permute-done.14 = f32[2,128,256]{2,1,0:T(8,128)S(1)} collective-permute-done((f32[2,128,256]{2,1,0:T(8,128)S(1)}, f32[2,128,256]{2,1,0:T(8,128)S(1)}, u32[]{:S(2)}, u32[]{:S(2)}) %collective-permute-start.14) | collective-permute-done | bytes 262176 | tf_op jit(solution)/shard_map/ppermute | solution.py:17
  207.1 3.1 %fusion.5 = f32[5,2,128,256]{3,1,2,0:T(2,128)S(1)} fusion(f32[5,2,128,256]{3,2,1,0:T(8,128)S(1)} %bitcast_dynamic-update-slice_fusion.5, s32[5,2]{1,0:T(8,128)S(1)} %stack.125, s32[5,2]{1,0:T(8,128)S(1)} %eq.126), kind=kOutput, calls=%fused_computation.14 | convolution fusion | flops 7864340 | bytes 2621520 | tf_op jit(solution)/shard_map/dml,dlbc->dmbc/dot_general | solution.py:63
  210.3 3.5 %convolution_bitcast_fusion.1 = f32[5,2,128,256]{2,3,1,0:T(8,128)} fusion(f32[5,2,128,128]{3,2,1,0:T(8,128)S(1)} %bitcast.140, f32[5,2,128,256]{3,1,2,0:T(2,128)S(1)} %fusion.5), kind=kOutput, calls=%fused_computation.1 | convolution fusion | flops 503316480 | bytes 3276800 | tf_op jit(solution)/shard_map/dmij,dmjc->dmic/dot_general | solution.py:64
  213.7 3.0 %copy.86 = f32[5,2,128,256]{3,0,1,2:T(8,128)} copy(f32[5,2,128,256]{2,3,1,0:T(8,128)} %convolution_bitcast_fusion.1) | data formatting | bytes 2621440 | tf_op jit(solution)/shard_map/dmij,dmjc->dmic/dot_general | solution.py:64
  216.7 2.4 fusion.10
  220.5 4.1 %collective-permute-start.20 = (f32[2,128,256]{2,1,0:T(8,128)S(1)}, f32[2,128,256]{2,1,0:T(8,128)S(1)}, u32[]{:S(2)}, u32[]{:S(2)}) collective-permute-start(f32[2,128,256]{2,1,0:T(8,128)S(1)} %get-tuple-element.26), channel_id=1, source_target_pairs={{511,0},{0,1},{1,2},{2,3},{3,4},{4,5},{5,6},{6,7},{7,8},{8,9},{9,1... | collective-permute-start | bytes 786440 | tf_op jit(solution)/shard_map/ppermute | solution.py:17
  224.5 1.9 collective-permute-start.21
  226.5 1.9 collective-permute-start.22
  228.4 2.2 collective-permute-start.23
  232.4 9.9 %collective-permute-done.21 = f32[2,128,256]{2,1,0:T(8,128)S(1)} collective-permute-done((f32[2,128,256]{2,1,0:T(8,128)S(1)}, f32[2,128,256]{2,1,0:T(8,128)S(1)}, u32[]{:S(2)}, u32[]{:S(2)}) %collective-permute-start.21) | collective-permute-done | bytes 262176 | tf_op jit(solution)/shard_map/ppermute | solution.py:17
  242.4 4.6 %collective-permute-done.22 = f32[2,128,256]{2,1,0:T(8,128)S(1)} collective-permute-done((f32[2,128,256]{2,1,0:T(8,128)S(1)}, f32[2,128,256]{2,1,0:T(8,128)S(1)}, u32[]{:S(2)}, u32[]{:S(2)}) %collective-permute-start.22) | collective-permute-done | bytes 262176 | tf_op jit(solution)/shard_map/ppermute | solution.py:17
  247.0 2.9 %collective-permute-done.23 = f32[2,128,256]{2,1,0:T(8,128)S(1)} collective-permute-done((f32[2,128,256]{2,1,0:T(8,128)S(1)}, f32[2,128,256]{2,1,0:T(8,128)S(1)}, u32[]{:S(2)}, u32[]{:S(2)}) %collective-permute-start.23) | collective-permute-done | bytes 262176 | tf_op jit(solution)/shard_map/ppermute | solution.py:17
  250.0 3.1 %fusion.3 = f32[5,2,128,256]{3,1,2,0:T(2,128)S(1)} fusion(f32[5,2,128,256]{3,2,1,0:T(8,128)S(1)} %bitcast_dynamic-update-slice_fusion, s32[5,2]{1,0:T(8,128)S(1)} %stack.137, s32[5,2]{1,0:T(8,128)S(1)} %eq.133), kind=kOutput, calls=%fused_computation.12 | convolution fusion | flops 7864340 | bytes 2621520 | tf_op jit(solution)/shard_map/dml,dlbc->dmbc/dot_general | solution.py:63
  253.1 2.4 convolution_bitcast_fusion
  255.5 2.0 copy.94
  257.6 2.4 fusion.11
  (95 shorter events, 35.9 us)
Async XLA Ops:
  0.0 1.1 copy-start
  0.9 26.8 %copy-start.13 = (s32[2]{0:T(128)}, s32[2]{0:T(128)S(1)}, u32[]{:S(2)}) copy-start(s32[2]{0:T(128)S(1)} %get-tuple-element.17) | copy-start | bytes 28
  0.9 28.1 %copy-start.11 = (s32[2]{0:T(128)}, s32[2]{0:T(128)S(1)}, u32[]{:S(2)}) copy-start(s32[2]{0:T(128)S(1)} %get-tuple-element.11) | copy-start | bytes 28
  0.9 166.4 %copy-start.15 = (s32[2]{0:T(128)}, s32[2]{0:T(128)S(1)}, u32[]{:S(2)}) copy-start(s32[2]{0:T(128)S(1)} %get-tuple-element.15) | copy-start | bytes 28
  4.2 21.1 %copy-start.5 = (f32[30,128,128]{2,1,0:T(8,128)S(1)}, f32[30,128,128]{2,1,0:T(8,128)}, u32[]{:S(2)}) copy-start(f32[30,128,128]{2,1,0:T(8,128)} %param.8) | copy-start | bytes 5898244
  4.6 148.0 %collective-permute-start.4 = (f32[2,128,256]{2,1,0:T(8,128)S(1)}, f32[2,128,256]{2,1,0:T(8,128)}, u32[]{:S(2)}, u32[]{:S(2)}) collective-permute-start(f32[2,128,256]{2,1,0:T(8,128)S(1)} %get-tuple-element.22), channel_id=1, source_target_pairs={{511,0},{0,1},{1,2},{2,3},{3,4},{4,5},{5,6},{6,7},{7,8},{8,9},{9,1... | collective-permute-start | bytes 786440 | tf_op jit(solution)/shard_map/ppermute | solution.py:17
  9.3 144.3 %collective-permute-start.5 = (f32[2,128,256]{2,1,0:T(8,128)S(1)}, f32[2,128,256]{2,1,0:T(8,128)}, u32[]{:S(2)}, u32[]{:S(2)}) collective-permute-start(f32[2,128,256]{2,1,0:T(8,128)S(1)} %get-tuple-element.22), channel_id=1, source_target_pairs={{510,0},{511,1},{0,2},{1,3},{2,4},{3,5},{4,6},{5,7},{6,8},{7,9},{8... | collective-permute-start | bytes 786440 | tf_op jit(solution)/shard_map/ppermute | solution.py:17
  12.5 142.0 %collective-permute-start.6 = (f32[2,128,256]{2,1,0:T(8,128)S(1)}, f32[2,128,256]{2,1,0:T(8,128)}, u32[]{:S(2)}, u32[]{:S(2)}) collective-permute-start(f32[2,128,256]{2,1,0:T(8,128)S(1)} %get-tuple-element.22), channel_id=1, source_target_pairs={{509,0},{510,1},{511,2},{0,3},{1,4},{2,5},{3,6},{4,7},{5,8},{6,9},... | collective-permute-start | bytes 786440 | tf_op jit(solution)/shard_map/ppermute | solution.py:17
  16.0 139.5 %collective-permute-start.7 = (f32[2,128,256]{2,1,0:T(8,128)S(1)}, f32[2,128,256]{2,1,0:T(8,128)}, u32[]{:S(2)}, u32[]{:S(2)}) collective-permute-start(f32[2,128,256]{2,1,0:T(8,128)S(1)} %get-tuple-element.22), channel_id=1, source_target_pairs={{508,0},{509,1},{510,2},{511,3},{0,4},{1,5},{2,6},{3,7},{4,8},{5,9... | collective-permute-start | bytes 786440 | tf_op jit(solution)/shard_map/ppermute | solution.py:17
  19.7 12.5 %collective-permute-start = (s32[2]{0:T(128)S(1)}, s32[2]{0:T(128)S(1)}, u32[]{:S(2)}, u32[]{:S(2)}) collective-permute-start(s32[2]{0:T(128)S(1)} %get-tuple-element.12), channel_id=1, source_target_pairs={{511,0},{0,1},{1,2},{2,3},{3,4},{4,5},{5,6},{6,7},{7,8},{8,9},{9,1... | collective-permute-start | bytes 32 | tf_op jit(solution)/shard_map/ppermute | solution.py:17
  25.3 1.0 copy-start.17
  26.3 4.1 %copy-start.16 = (s32[30]{0:T(128)S(1)}, s32[30]{0:T(128)}, u32[]{:S(2)}) copy-start(s32[30]{0:T(128)} %param.11) | copy-start | bytes 364
  32.1 12.8 %collective-permute-start.1 = (s32[2]{0:T(128)S(1)}, s32[2]{0:T(128)S(1)}, u32[]{:S(2)}, u32[]{:S(2)}) collective-permute-start(s32[2]{0:T(128)S(1)} %get-tuple-element.12), channel_id=1, source_target_pairs={{510,0},{511,1},{0,2},{1,3},{2,4},{3,5},{4,6},{5,7},{6,8},{7,9},{8... | collective-permute-start | bytes 32 | tf_op jit(solution)/shard_map/ppermute | solution.py:17
  44.9 11.7 %collective-permute-start.2 = (s32[2]{0:T(128)S(1)}, s32[2]{0:T(128)S(1)}, u32[]{:S(2)}, u32[]{:S(2)}) collective-permute-start(s32[2]{0:T(128)S(1)} %get-tuple-element.12), channel_id=1, source_target_pairs={{509,0},{510,1},{511,2},{0,3},{1,4},{2,5},{3,6},{4,7},{5,8},{6,9},... | collective-permute-start | bytes 32 | tf_op jit(solution)/shard_map/ppermute | solution.py:17
  56.6 10.0 %collective-permute-start.3 = (s32[2]{0:T(128)S(1)}, s32[2]{0:T(128)S(1)}, u32[]{:S(2)}, u32[]{:S(2)}) collective-permute-start(s32[2]{0:T(128)S(1)} %get-tuple-element.12), channel_id=1, source_target_pairs={{508,0},{509,1},{510,2},{511,3},{0,4},{1,5},{2,6},{3,7},{4,8},{5,9... | collective-permute-start | bytes 32 | tf_op jit(solution)/shard_map/ppermute | solution.py:17
  66.6 11.8 %collective-permute-start.8 = (s32[2]{0:T(128)S(1)}, s32[2]{0:T(128)S(1)}, u32[]{:S(2)}, u32[]{:S(2)}) collective-permute-start(s32[2]{0:T(128)S(1)} %get-tuple-element.13), channel_id=1, source_target_pairs={{511,0},{0,1},{1,2},{2,3},{3,4},{4,5},{5,6},{6,7},{7,8},{8,9},{9,1... | collective-permute-start | bytes 32 | tf_op jit(solution)/shard_map/ppermute | solution.py:17
  78.4 9.7 %collective-permute-start.9 = (s32[2]{0:T(128)S(1)}, s32[2]{0:T(128)S(1)}, u32[]{:S(2)}, u32[]{:S(2)}) collective-permute-start(s32[2]{0:T(128)S(1)} %get-tuple-element.13), channel_id=1, source_target_pairs={{510,0},{511,1},{0,2},{1,3},{2,4},{3,5},{4,6},{5,7},{6,8},{7,9},{8... | collective-permute-start | bytes 32 | tf_op jit(solution)/shard_map/ppermute | solution.py:17
  88.1 11.4 %collective-permute-start.10 = (s32[2]{0:T(128)S(1)}, s32[2]{0:T(128)S(1)}, u32[]{:S(2)}, u32[]{:S(2)}) collective-permute-start(s32[2]{0:T(128)S(1)} %get-tuple-element.13), channel_id=1, source_target_pairs={{509,0},{510,1},{511,2},{0,3},{1,4},{2,5},{3,6},{4,7},{5,8},{6,9},... | collective-permute-start | bytes 32 | tf_op jit(solution)/shard_map/ppermute | solution.py:17
  99.6 10.0 %collective-permute-start.11 = (s32[2]{0:T(128)S(1)}, s32[2]{0:T(128)S(1)}, u32[]{:S(2)}, u32[]{:S(2)}) collective-permute-start(s32[2]{0:T(128)S(1)} %get-tuple-element.13), channel_id=1, source_target_pairs={{508,0},{509,1},{510,2},{511,3},{0,4},{1,5},{2,6},{3,7},{4,8},{5,9... | collective-permute-start | bytes 32 | tf_op jit(solution)/shard_map/ppermute | solution.py:17
  109.6 11.8 %collective-permute-start.16 = (s32[2]{0:T(128)S(1)}, s32[2]{0:T(128)S(1)}, u32[]{:S(2)}, u32[]{:S(2)}) collective-permute-start(s32[2]{0:T(128)S(1)} %get-tuple-element.14), channel_id=1, source_target_pairs={{511,0},{0,1},{1,2},{2,3},{3,4},{4,5},{5,6},{6,7},{7,8},{8,9},{9,1... | collective-permute-start | bytes 32 | tf_op jit(solution)/shard_map/ppermute | solution.py:17
  121.4 9.7 %collective-permute-start.17 = (s32[2]{0:T(128)S(1)}, s32[2]{0:T(128)S(1)}, u32[]{:S(2)}, u32[]{:S(2)}) collective-permute-start(s32[2]{0:T(128)S(1)} %get-tuple-element.14), channel_id=1, source_target_pairs={{510,0},{511,1},{0,2},{1,3},{2,4},{3,5},{4,6},{5,7},{6,8},{7,9},{8... | collective-permute-start | bytes 32 | tf_op jit(solution)/shard_map/ppermute | solution.py:17
  131.1 11.4 %collective-permute-start.18 = (s32[2]{0:T(128)S(1)}, s32[2]{0:T(128)S(1)}, u32[]{:S(2)}, u32[]{:S(2)}) collective-permute-start(s32[2]{0:T(128)S(1)} %get-tuple-element.14), channel_id=1, source_target_pairs={{509,0},{510,1},{511,2},{0,3},{1,4},{2,5},{3,6},{4,7},{5,8},{6,9},... | collective-permute-start | bytes 32 | tf_op jit(solution)/shard_map/ppermute | solution.py:17
  142.5 10.0 %collective-permute-start.19 = (s32[2]{0:T(128)S(1)}, s32[2]{0:T(128)S(1)}, u32[]{:S(2)}, u32[]{:S(2)}) collective-permute-start(s32[2]{0:T(128)S(1)} %get-tuple-element.14), channel_id=1, source_target_pairs={{508,0},{509,1},{510,2},{511,3},{0,4},{1,5},{2,6},{3,7},{4,8},{5,9... | collective-permute-start | bytes 32 | tf_op jit(solution)/shard_map/ppermute | solution.py:17
  167.3 0.9 copy-start.8
  167.3 13.8 %copy-start.1 = (f32[8,128,256]{2,0,1:T(8,128)S(1)}, f32[8,128,256]{2,0,1:T(8,128)}, u32[]{:S(2)}) copy-start(f32[8,128,256]{2,0,1:T(8,128)} %fusion.31) | copy-start | bytes 3145732
  168.6 15.1 %collective-permute-start.12 = (f32[2,128,256]{2,1,0:T(8,128)S(1)}, f32[2,128,256]{2,1,0:T(8,128)S(1)}, u32[]{:S(2)}, u32[]{:S(2)}) collective-permute-start(f32[2,128,256]{2,1,0:T(8,128)S(1)} %get-tuple-element.24), channel_id=1, source_target_pairs={{511,0},{0,1},{1,2},{2,3},{3,4},{4,5},{5,6},{6,7},{7,8},{8,9},{9,1... | collective-permute-start | bytes 786440 | tf_op jit(solution)/shard_map/ppermute | solution.py:17
  173.9 25.3 %collective-permute-start.13 = (f32[2,128,256]{2,1,0:T(8,128)S(1)}, f32[2,128,256]{2,1,0:T(8,128)S(1)}, u32[]{:S(2)}, u32[]{:S(2)}) collective-permute-start(f32[2,128,256]{2,1,0:T(8,128)S(1)} %get-tuple-element.24), channel_id=1, source_target_pairs={{510,0},{511,1},{0,2},{1,3},{2,4},{3,5},{4,6},{5,7},{6,8},{7,9},{8... | collective-permute-start | bytes 786440 | tf_op jit(solution)/shard_map/ppermute | solution.py:17
  176.7 28.6 %collective-permute-start.14 = (f32[2,128,256]{2,1,0:T(8,128)S(1)}, f32[2,128,256]{2,1,0:T(8,128)S(1)}, u32[]{:S(2)}, u32[]{:S(2)}) collective-permute-start(f32[2,128,256]{2,1,0:T(8,128)S(1)} %get-tuple-element.24), channel_id=1, source_target_pairs={{509,0},{510,1},{511,2},{0,3},{1,4},{2,5},{3,6},{4,7},{5,8},{6,9},... | collective-permute-start | bytes 786440 | tf_op jit(solution)/shard_map/ppermute | solution.py:17
  179.0 28.1 %collective-permute-start.15 = (f32[2,128,256]{2,1,0:T(8,128)S(1)}, f32[2,128,256]{2,1,0:T(8,128)S(1)}, u32[]{:S(2)}, u32[]{:S(2)}) collective-permute-start(f32[2,128,256]{2,1,0:T(8,128)S(1)} %get-tuple-element.24), channel_id=1, source_target_pairs={{508,0},{509,1},{510,2},{511,3},{0,4},{1,5},{2,6},{3,7},{4,8},{5,9... | collective-permute-start | bytes 786440 | tf_op jit(solution)/shard_map/ppermute | solution.py:17
  207.1 3.2 %copy-start.4 = (f32[10,128,128]{2,1,0:T(8,128)S(1)}, f32[10,128,128]{2,1,0:T(8,128)}, u32[]{:S(2)}) copy-start(f32[10,128,128]{2,1,0:T(8,128)} %get-tuple-element.7) | copy-start | bytes 1966084
  213.7 3.0 %copy-start.10 = (pred[5,2,8]{0,2,1:T(8,128)(4,1)S(1)}, pred[5,2,8]{0,2,1:T(8,128)(4,1)}, u32[]{:S(2)}) copy-start(pred[5,2,8]{0,2,1:T(8,128)(4,1)} %copy.85) | copy-start | bytes 244
  216.7 2.4 copy-start.14
  219.2 0.9 copy-start.7
  219.2 11.4 %copy-start.2 = (f32[8,128,256]{2,0,1:T(8,128)S(1)}, f32[8,128,256]{2,0,1:T(8,128)}, u32[]{:S(2)}) copy-start(f32[8,128,256]{2,0,1:T(8,128)} %convolution_add_fusion.2) | copy-start | bytes 3145732
  220.5 12.0 %collective-permute-start.20 = (f32[2,128,256]{2,1,0:T(8,128)S(1)}, f32[2,128,256]{2,1,0:T(8,128)S(1)}, u32[]{:S(2)}, u32[]{:S(2)}) collective-permute-start(f32[2,128,256]{2,1,0:T(8,128)S(1)} %get-tuple-element.26), channel_id=1, source_target_pairs={{511,0},{0,1},{1,2},{2,3},{3,4},{4,5},{5,6},{6,7},{7,8},{8,9},{9,1... | collective-permute-start | bytes 786440 | tf_op jit(solution)/shard_map/ppermute | solution.py:17
  224.5 17.9 %collective-permute-start.21 = (f32[2,128,256]{2,1,0:T(8,128)S(1)}, f32[2,128,256]{2,1,0:T(8,128)S(1)}, u32[]{:S(2)}, u32[]{:S(2)}) collective-permute-start(f32[2,128,256]{2,1,0:T(8,128)S(1)} %get-tuple-element.26), channel_id=1, source_target_pairs={{510,0},{511,1},{0,2},{1,3},{2,4},{3,5},{4,6},{5,7},{6,8},{7,9},{8... | collective-permute-start | bytes 786440 | tf_op jit(solution)/shard_map/ppermute | solution.py:17
  226.5 20.6 %collective-permute-start.22 = (f32[2,128,256]{2,1,0:T(8,128)S(1)}, f32[2,128,256]{2,1,0:T(8,128)S(1)}, u32[]{:S(2)}, u32[]{:S(2)}) collective-permute-start(f32[2,128,256]{2,1,0:T(8,128)S(1)} %get-tuple-element.26), channel_id=1, source_target_pairs={{509,0},{510,1},{511,2},{0,3},{1,4},{2,5},{3,6},{4,7},{5,8},{6,9},... | collective-permute-start | bytes 786440 | tf_op jit(solution)/shard_map/ppermute | solution.py:17
  228.4 21.6 %collective-permute-start.23 = (f32[2,128,256]{2,1,0:T(8,128)S(1)}, f32[2,128,256]{2,1,0:T(8,128)S(1)}, u32[]{:S(2)}, u32[]{:S(2)}) collective-permute-start(f32[2,128,256]{2,1,0:T(8,128)S(1)} %get-tuple-element.26), channel_id=1, source_target_pairs={{508,0},{509,1},{510,2},{511,3},{0,4},{1,5},{2,6},{3,7},{4,8},{5,9... | collective-permute-start | bytes 786440 | tf_op jit(solution)/shard_map/ppermute | solution.py:17
  255.5 2.0 copy-start.9
  257.5 2.4 copy-start.12
  260.0 0.9 copy-start.6
  260.0 1.3 copy-start.3
where the time goes:
time: 265 us; the launch traced here: 263 us
  waiting for transfers between devices  133 us (50%)
  starting transfers between devices  69.9 us (26%)
  matrix products  43.2 us (16%)
  local copies, waits for them, and re-layouts  16.2 us (6%)
    ppermute x24, waiting for transfers between devices, from_behind(): return lax.ppermute(block, axis, route)  133 us
    ppermute x24, starting transfers between devices, from_behind(): return lax.ppermute(block, axis, route)  69.9 us
    dot_general x3, matrix products, body(): jnp.einsum('dml,dlbc->dmbc', matches, stacked_values, precision=HIGH)  9.41 us
    dot_general x8, matrix products, select_rows(): return jnp.einsum('ar,rbc->abc', picker, stacked, precision=HIGH)  8.92 us
    dot_general x3, matrix products, body(): jnp.einsum('dmij,dmjc->dmic', blocks_now, inputs, precision=HIGH)  8.25 us
    dot_general x3, matrix products, body(): jnp.einsum('dmr,dmic->ric', landing, product_terms, precision=HIGH)  8.08 us
    dot_general x4, matrix products, body(): jnp.einsum('lr,lbc->rbc', picker, solved, precision=HIGH)  7.03 us
    dot_general x3, local copies, waits for them, and re-layouts, body(): jnp.einsum('dmij,dmjc->dmic', blocks_now, inputs, precision=HIGH)  7 us
  transfers between devices with their start and end apart: 24, of which 17 were waited for; matrix products, arithmetic and copies ran while one was open for 6% of the time, Pallas kernels for 0%

commit v1 on v0

v1 whole, which is shorter than its diff:
```python
import jax
import jax.numpy as jnp
from jax import lax
from jax.experimental import pallas as pl
from jax.experimental.pallas import tpu as pltpu
from jax.sharding import PartitionSpec as P

BS = 128
RHS = 256
LANES = 2
STEPS = 4
BAND = 4
R = 8
GROUP = (BAND + 1) * LANES

VMEM = pl.BlockSpec(memory_space=pltpu.VMEM)
SMEM = pl.BlockSpec(memory_space=pltpu.SMEM)
ANY = pl.BlockSpec(memory_space=pl.ANY)
HBM = pl.BlockSpec(memory_space=pltpu.HBM)


def halves(value):
    high = value.astype(jnp.bfloat16)
    low = (value - high.astype(jnp.float32)).astype(jnp.bfloat16)
    return high, low


def left(value):
    high, low = halves(value)
    return jnp.concatenate([high, high, low], axis=1)


def right(value):
    high, low = halves(value)
    return jnp.concatenate([high, low, high], axis=0)


def dot(a, b):
    return jnp.dot(a, b, preferred_element_type=jnp.float32)


def slot_at(order, p):
    a, b = order[p - p % 2], order[p - p % 2 + 1]
    return jnp.maximum(a, b) if p % 2 else jnp.minimum(a, b)


def block_of(blk_col, step, offset, lane):
    first = step * GROUP + offset * LANES
    swapped = (blk_col[first] > blk_col[first + 1]).astype(jnp.int32)
    return first + (swapped if lane == 0 else 1 - swapped)


def weights(order, blk_row, blk_col, f_ref, blocks, positions):
    slots = [slot_at(order, p) for p in positions]
    columns = []
    for step, offset, lane in blocks:
        j = block_of(blk_col, step, offset, lane)
        own = left(f_ref[j])
        row = lax.rem(blk_row[j], R)
        columns.append(
            jnp.concatenate(
                [jnp.where(row == s, own, jnp.zeros_like(own)) for s in slots], axis=0
            )
        )
    return columns


def spread(order, blk_row, blk_col, f_ref, terms, positions):
    columns = weights(order, blk_row, blk_col, f_ref, [t[:3] for t in terms], positions)
    return dot(
        jnp.concatenate(columns, axis=1),
        jnp.concatenate([right(t[3]) for t in terms], axis=0),
    )


def copies(pairs, sems):
    made = [pltpu.make_async_copy(s, d, sems.at[i]) for i, (s, d) in enumerate(pairs)]
    for c in made:
        c.start()
    return made


def first_kernel(order, rhs, diag, x_ref, res, inv, sems):
    pairs = []
    for lane in range(LANES):
        slot = slot_at(order, lane)
        pairs += [(rhs.at[slot], res.at[lane]), (diag.at[slot], inv.at[lane])]
    made = copies(pairs, sems)
    for c in made:
        c.wait()
    for lane in range(LANES):
        x_ref[lane] = dot(left(inv[lane]), right(res[lane]))


def solve_kernel(step, order, blk_row, blk_col, f_ref, diag, res, far2, far4, near, *rest):
    if step == STEPS - 1:
        _, out, x_ref, inv, sems, out_sems = rest
    else:
        x_ref, inv, sems = rest
    slots = [slot_at(order, step * LANES + lane) for lane in range(LANES)]
    made = copies([(diag.at[slots[l]], inv.at[l]) for l in range(LANES)], sems)
    sources = {1: near.at[0], 2: far2, 3: near.at[1], 4: far4}
    terms = [
        (step - 1, e, lane, sources[e][lane])
        for e in range(1, BAND + 1)
        for lane in range(LANES)
    ]
    positions = range(step * LANES, (step + 1) * LANES)
    total = spread(order, blk_row, blk_col, f_ref, terms, positions)
    base = res.shape[0] - (R - step * LANES)
    for c in made:
        c.wait()
    for lane in range(LANES):
        rest_of = res[base + lane] - total[lane * BS : (lane + 1) * BS]
        x_ref[lane] = dot(left(inv[lane]), right(rest_of))
    if step == STEPS - 1:
        made = copies([(x_ref.at[l], out.at[slots[l]]) for l in range(LANES)], out_sems)
        for c in made:
            c.wait()


def window_kernel(step, order, blk_row, blk_col, f_ref, x_ref, *rest):
    slots = [slot_at(order, step * LANES + lane) for lane in range(LANES)]
    if step == 0:
        rhs, out, new, res, sems, out_sems = rest
        made = copies(
            [(rhs.at[slot_at(order, p)], res.at[p - LANES]) for p in range(LANES, R)], sems
        )
        base = 0
        terms = []
    else:
        res, far2, far4, near, _, out, new, out_sems = rest
        made = []
        base = LANES
        sources = {1: near.at[0], 2: far2, 3: near.at[1], 4: far4}
        terms = [
            (step - 1, e, lane, sources[e][lane])
            for e in range(1, BAND + 1)
            for lane in range(LANES)
        ]
    out_made = copies([(x_ref.at[l], out.at[slots[l]]) for l in range(LANES)], out_sems)
    terms += [(step, 0, lane, x_ref[lane]) for lane in range(LANES)]
    positions = range((step + 1) * LANES, R)
    total = spread(order, blk_row, blk_col, f_ref, terms, positions)
    for c in made:
        c.wait()
    for i in range(len(positions)):
        new[i] = res[base + i] - total[i * BS : (i + 1) * BS]
    for c in out_made:
        c.wait()


def body(rhs, diag_inv, factor_blocks, order, blk_row, blk_col):
    f32 = jnp.float32
    rhs = rhs.reshape(R, BS, RHS)
    diag = diag_inv.reshape(R, BS, BS)
    count = lax.axis_size("blk")
    odd = lax.rem(lax.axis_index("blk"), 2) == 1
    pair = jax.ShapeDtypeStruct((LANES, BS, RHS), f32)
    whole = jax.ShapeDtypeStruct((R, BS, RHS), f32)
    dma = pltpu.SemaphoreType.DMA
    params = pltpu.CompilerParams(vmem_limit_bytes=24 << 20)

    def shift(value, distance):
        return lax.ppermute(value, "blk", [(i, (i + distance) % count) for i in range(count)])

    def swap(value):
        return lax.ppermute(value, "blk", [(i, i ^ 1) for i in range(count)])

    def cost(blocks, rows):
        return pl.CostEstimate(
            flops=6 * blocks * rows * BS * BS * RHS, bytes_accessed=3 << 20, transcendentals=0
        )

    x = pl.pallas_call(
        first_kernel,
        out_shape=pair,
        in_specs=[SMEM, HBM, HBM],
        out_specs=VMEM,
        scratch_shapes=[
            pltpu.VMEM((LANES, BS, RHS), f32),
            pltpu.VMEM((LANES, BS, BS), f32),
            dma((2 * LANES,)),
        ],
        compiler_params=params,
        name="first",
    )(order, rhs, diag)
    far2 = shift(x, 2)
    far4 = shift(x, 4)
    res, near, out = None, None, None
    last = None
    for step in range(STEPS - 1):
        later = R - (step + 1) * LANES
        new_shape = jax.ShapeDtypeStruct((later, BS, RHS), f32)

        def window(*args, step=step):
            return window_kernel(step, *args)

        if step == 0:
            out, res = pl.pallas_call(
                window,
                out_shape=(whole, new_shape),
                in_specs=[SMEM] * 3 + [VMEM, VMEM, ANY],
                out_specs=(ANY, VMEM),
                scratch_shapes=[
                    pltpu.VMEM((R - LANES, BS, RHS), f32),
                    dma((R - LANES,)),
                    dma((LANES,)),
                ],
                compiler_params=params,
                cost_estimate=cost(2, 6),
                name="window0",
            )(order, blk_row, blk_col, factor_blocks, x, rhs)
        else:
            out, res = pl.pallas_call(
                window,
                out_shape=(whole, new_shape),
                in_specs=[SMEM] * 3 + [VMEM] * 6 + [ANY],
                out_specs=(ANY, VMEM),
                scratch_shapes=[dma((LANES,))],
                input_output_aliases={9: 0},
                compiler_params=params,
                cost_estimate=cost(10, R - (step + 1) * LANES),
                name=f"window{step}",
            )(order, blk_row, blk_col, factor_blocks, x, res, *last, out)
        x, res = lax.optimization_barrier((x, res))
        payload = jnp.where(odd, jnp.stack([far2, far4]), jnp.stack([x, far2]))
        near = swap(payload)
        last = (far2, far4, near)

        def solve(*args, step=step + 1):
            return solve_kernel(step, *args)

        end = step + 1 == STEPS - 1
        scratch = [pltpu.VMEM((LANES, BS, BS), f32), dma((LANES,))]
        if end:
            scratch = [pltpu.VMEM((LANES, BS, RHS), f32)] + scratch + [dma((LANES,))]
        got = pl.pallas_call(
            solve,
            out_shape=whole if end else pair,
            in_specs=[SMEM] * 3 + [VMEM, ANY] + [VMEM] * 4 + ([ANY] if end else []),
            out_specs=ANY if end else VMEM,
            scratch_shapes=scratch,
            input_output_aliases={9: 0} if end else {},
            compiler_params=params,
            name=f"solve{step + 1}",
        )(order, blk_row, blk_col, factor_blocks, diag, res, *last, *([out] if end else []))
        if end:
            return got.reshape(R * BS, RHS)
        x = got
        far2 = shift(x, 2)
        far4 = shift(x, 4)


def solution(mesh):
    placed = (P("blk", None), P("blk", None), P("blk", None, None), P("blk"), P("blk"), P("blk"))
    return jax.shard_map(
        body, mesh=mesh, in_specs=placed, out_specs=P("blk", None), check_vma=False
    )
```

time: 265 us -> 94.8 us (0.36)
  waiting for transfers between devices: 133 us -> 48 us
  starting transfers between devices: 69.9 us -> 26 us
  matrix products: 43.2 us -> 0 us
  Pallas kernels: 0 us -> 13.5 us
  local copies, waits for them, and re-layouts: 16.2 us -> 6.45 us
    ppermute x24 -> x9, waiting for transfers between devices: 133 us -> 48 us  [the longest x6 43.5 us: shift(): lax.ppermute(value, 'blk', [(i, (i + distance) % count) for i in range(co...]
    ppermute x24 -> x9, starting transfers between devices: 69.9 us -> 26 us  [the longest x6 15.6 us: shift(): lax.ppermute(value, 'blk', [(i, (i + distance) % count) for i in range(co...]
    dot_general x25 -> x0, matrix products: 43.2 us -> none  [the longest x3 9.41 us: body(): jnp.einsum('dml,dlbc->dmbc', matches, stacked_values, precision=HIGH)]
    pallas_call x0 -> x7, Pallas kernels: none -> 13.5 us  [the longest x3 6.3 us: body(): pl.pallas_call(window, out_shape=(whole, new_shape), in_specs=[SMEM] * 3...]
    dot_general x3 -> x0, local copies, waits for them, and re-layouts: 7 us -> none  [body(): jnp.einsum('dmij,dmjc->dmic', blocks_now, inputs, precision=HIGH)]
    unnamed x45 -> x26, local copies, waits for them, and re-layouts: 4.04 us -> 6.45 us
  transfers between devices with their start and end apart: 24 -> 9, of which waited for: 17 -> 9; matrix products, arithmetic and copies ran while one was open for 6% -> 0% of each run, Pallas kernels for 0% -> 7%
where the time goes in v1:
time: 94.8 us; the launch traced here: 94.3 us
  waiting for transfers between devices  48 us (51%)
  starting transfers between devices  26 us (27%)
  Pallas kernels  13.5 us (14%)
  local copies, waits for them, and re-layouts  6.45 us (7%)
    ppermute x6, waiting for transfers between devices, shift(): lax.ppermute(value, 'blk', [(i, (i + distance) % count) for i in range(co...  43.5 us
    ppermute x6, starting transfers between devices, shift(): lax.ppermute(value, 'blk', [(i, (i + distance) % count) for i in range(co...  15.6 us
    ppermute x3, starting transfers between devices, swap(): return lax.ppermute(value, 'blk', [(i, i ^ 1) for i in range(count)])  10.3 us
    unnamed x26, local copies, waits for them, and re-layouts  6.45 us
    pallas_call x3, Pallas kernels, body(): pl.pallas_call(window, out_shape=(whole, new_shape), in_specs=[SMEM] * 3...  6.3 us
    pallas_call x3, Pallas kernels, body(): pl.pallas_call(solve, out_shape=whole if end else pair, in_specs=[SMEM] *...  5.84 us
    ppermute x3, waiting for transfers between devices, swap(): return lax.ppermute(value, 'blk', [(i, i ^ 1) for i in range(count)])  4.54 us
  transfers between devices with their start and end apart: 9, of which 9 were waited for; matrix products, arithmetic and copies ran while one was open for 0% of the time, Pallas kernels for 7%

profile of v1, /device:TPU:1, one launch (start us, length us, event | category | flops | bytes accessed | tf_op | source)
XLA Modules:
  0.0 94.3 jit_solution(16193855077820036442)
XLA Ops:
  0.0 0.0 copy-start.2
  0.0 1.0 %copy-done.2 = f32[1024,128]{1,0:T(8,128)S(1)} copy-done((f32[1024,128]{1,0:T(8,128)S(1)}, f32[1024,128]{1,0:T(8,128)}, u32[]{:S(2)}) %copy-start.2) | copy-done | bytes 524312
  1.0 0.0 copy-start.4
  1.0 1.2 %copy-done.4 = f32[1024,256]{1,0:T(8,128)S(1)} copy-done((f32[1024,256]{1,0:T(8,128)S(1)}, f32[1024,256]{1,0:T(8,128)}, u32[]{:S(2)}) %copy-start.4) | copy-done | bytes 1048600
  2.3 0.0 copy-start.6
  2.3 0.7 copy-done.6
  2.9 1.3 %first.1.args_4_ = f32[2,128,256]{2,1,0:T(8,128)S(1)} custom-call(s32[8]{0:T(128)S(1)} %copy-done.6, f32[8,128,256]{2,1,0:T(8,128)S(1)} %bitcast.16, f32[8,128,128]{2,1,0:T(8,128)S(1)} %bitcast.12), custom_call_target="tpu_custom_call" | custom-call | tf_op jit(solution)/shard_map/first/pallas_call | solution.py:175
  4.3 5.6 %collective-permute-start.1 = (f32[2,128,256]{2,1,0:T(8,128)S(1)}, f32[2,128,256]{2,1,0:T(8,128)S(1)}, u32[]{:S(2)}, u32[]{:S(2)}) collective-permute-start(f32[2,128,256]{2,1,0:T(8,128)S(1)} %first.1.args_4_), channel_id=1, source_target_pairs={{0,4},{1,5},{2,6},{3,7},{4,8},{5,9},{6,10},{7,11},{8,12},{9,13},{1... | collective-permute-start | bytes 786440 | tf_op jit(solution)/shard_map/ppermute | solution.py:165
  9.9 2.3 %collective-permute-start = (f32[2,128,256]{2,1,0:T(8,128)S(1)}, f32[2,128,256]{2,1,0:T(8,128)S(1)}, u32[]{:S(2)}, u32[]{:S(2)}) collective-permute-start(f32[2,128,256]{2,1,0:T(8,128)S(1)} %first.1.args_4_), channel_id=1, source_target_pairs={{0,2},{1,3},{2,4},{3,5},{4,6},{5,7},{6,8},{7,9},{8,10},{9,11},{10,... | collective-permute-start | bytes 786440 | tf_op jit(solution)/shard_map/ppermute | solution.py:165
  12.2 0.0 copy-done.5
  12.2 0.0 copy-start
  12.3 1.5 %copy-done = f32[30,128,128]{2,1,0:T(8,128)S(1)} copy-done((f32[30,128,128]{2,1,0:T(8,128)S(1)}, f32[30,128,128]{2,1,0:T(8,128)}, u32[]{:S(2)}) %copy-start) | copy-done | bytes 1966104
  13.8 0.7 copy-done.7
  14.4 0.7 copy-done.9
  15.1 0.7 copy-done.11
  15.8 2.4 %window0.1 = (f32[8,128,256]{2,1,0:T(8,128)}, f32[6,128,256]{2,1,0:T(8,128)S(1)}) custom-call(s32[8]{0:T(128)S(1)} %copy-done.7, s32[30]{0:T(128)S(1)} %copy-done.9, s32[30]{0:T(128)S(1)} %copy-done.11, f32[30,128,128]{2,1,0:T(8,128)S(1)} %copy-done, f32[2,128,256]{2,1,0:T(8,128)S(1)} %first.1.args_4_, f32[8,128,256]{2,1,0:T(8,128)S(1)} %bitcast.17), custom_call_target="tpu_custom_call" | custom-call | flops 301989888 | bytes 3145728 | tf_op jit(solution)/shard_map/window0/pallas_call | solution.py:200
  18.2 8.8 %collective-permute-done.1.args_7_ = f32[2,128,256]{2,1,0:T(8,128)S(1)} collective-permute-done((f32[2,128,256]{2,1,0:T(8,128)S(1)}, f32[2,128,256]{2,1,0:T(8,128)S(1)}, u32[]{:S(2)}, u32[]{:S(2)}) %collective-permute-start.1) | collective-permute-done | bytes 262176 | tf_op jit(solution)/shard_map/ppermute | solution.py:165
  27.0 5.4 %collective-permute-done.args_6_ = f32[2,128,256]{2,1,0:T(8,128)S(1)} collective-permute-done((f32[2,128,256]{2,1,0:T(8,128)S(1)}, f32[2,128,256]{2,1,0:T(8,128)S(1)}, u32[]{:S(2)}, u32[]{:S(2)}) %collective-permute-start) | collective-permute-done | bytes 262176 | tf_op jit(solution)/shard_map/ppermute | solution.py:165
  32.5 0.1 maximum_select_fusion
  32.5 3.3 %collective-permute-start.2 = (f32[2,2,128,256]{3,2,1,0:T(8,128)S(1)}, f32[2,2,128,256]{3,2,1,0:T(8,128)S(1)}, u32[]{:S(2)}, u32[]{:S(2)}) collective-permute-start(f32[2,2,128,256]{3,2,1,0:T(8,128)S(1)} %maximum_select_fusion), channel_id=1, source_target_pairs={{0,1},{1,0},{2,3},{3,2},{4,5},{5,4},{6,7},{7,6},{8,9},{9,8},{10,11... | collective-permute-start | bytes 1572872 | tf_op jit(solution)/shard_map/ppermute | solution.py:168
  35.9 1.5 %collective-permute-done.2.args_8_ = f32[2,2,128,256]{3,2,1,0:T(8,128)S(1)} collective-permute-done((f32[2,2,128,256]{3,2,1,0:T(8,128)S(1)}, f32[2,2,128,256]{3,2,1,0:T(8,128)S(1)}, u32[]{:S(2)}, u32[]{:S(2)}) %collective-permute-start.2) | collective-permute-done | bytes 524320 | tf_op jit(solution)/shard_map/ppermute | solution.py:168
  37.4 0.0 copy-done.1
  37.4 0.0 copy-done.3
  37.4 1.7 %solve1.1.args_4_ = f32[2,128,256]{2,1,0:T(8,128)S(1)} custom-call(s32[8]{0:T(128)S(1)} %copy-done.7, s32[30]{0:T(128)S(1)} %copy-done.9, s32[30]{0:T(128)S(1)} %copy-done.11, f32[30,128,128]{2,1,0:T(8,128)S(1)} %copy-done.1, f32[8,128,128]{2,1,0:T(8,128)S(1)} %bitcast.13, f32[6,128,256]{2,1,0:T(8,128)S(1)} %get-tuple-element.18.args_5_, ...), custom_call_target="tpu_custom_call" | custom-call | tf_op jit(solution)/shard_map/solve1/pallas_call | solution.py:238
  39.1 1.9 %collective-permute-start.4 = (f32[2,128,256]{2,1,0:T(8,128)S(1)}, f32[2,128,256]{2,1,0:T(8,128)S(1)}, u32[]{:S(2)}, u32[]{:S(2)}) collective-permute-start(f32[2,128,256]{2,1,0:T(8,128)S(1)} %solve1.1.args_4_), channel_id=1, source_target_pairs={{0,4},{1,5},{2,6},{3,7},{4,8},{5,9},{6,10},{7,11},{8,12},{9,13},{1... | collective-permute-start | bytes 786440 | tf_op jit(solution)/shard_map/ppermute | solution.py:165
  41.0 1.9 %collective-permute-start.3 = (f32[2,128,256]{2,1,0:T(8,128)S(1)}, f32[2,128,256]{2,1,0:T(8,128)S(1)}, u32[]{:S(2)}, u32[]{:S(2)}) collective-permute-start(f32[2,128,256]{2,1,0:T(8,128)S(1)} %solve1.1.args_4_), channel_id=1, source_target_pairs={{0,2},{1,3},{2,4},{3,5},{4,6},{5,7},{6,8},{7,9},{8,10},{9,11},{10,... | collective-permute-start | bytes 786440 | tf_op jit(solution)/shard_map/ppermute | solution.py:165
  43.0 2.2 %window1.1 = (f32[8,128,256]{2,1,0:T(8,128)}, f32[4,128,256]{2,1,0:T(8,128)S(1)}) custom-call(s32[8]{0:T(128)S(1)} %copy-done.7, s32[30]{0:T(128)S(1)} %copy-done.9, s32[30]{0:T(128)S(1)} %copy-done.11, f32[30,128,128]{2,1,0:T(8,128)S(1)} %copy-done.1, f32[2,128,256]{2,1,0:T(8,128)S(1)} %solve1.1.args_4_, ...), custom_call_target="tpu_custom_call", output_to_operand_aliasing={{0}: (9, {})} | custom-call | flops 1006632960 | bytes 3145728 | tf_op jit(solution)/shard_map/window1/pallas_call | solution.py:215
  45.2 12.5 %collective-permute-done.4.args_7_ = f32[2,128,256]{2,1,0:T(8,128)S(1)} collective-permute-done((f32[2,128,256]{2,1,0:T(8,128)S(1)}, f32[2,128,256]{2,1,0:T(8,128)S(1)}, u32[]{:S(2)}, u32[]{:S(2)}) %collective-permute-start.4) | collective-permute-done | bytes 262176 | tf_op jit(solution)/shard_map/ppermute | solution.py:165
  57.7 1.9 %collective-permute-done.3.args_6_ = f32[2,128,256]{2,1,0:T(8,128)S(1)} collective-permute-done((f32[2,128,256]{2,1,0:T(8,128)S(1)}, f32[2,128,256]{2,1,0:T(8,128)S(1)}, u32[]{:S(2)}, u32[]{:S(2)}) %collective-permute-start.3) | collective-permute-done | bytes 262176 | tf_op jit(solution)/shard_map/ppermute | solution.py:165
  59.5 0.1 maximum_select_fusion.1
  59.6 0.0 copy-start.8
  59.6 0.0 copy-start.10
  59.6 0.0 copy-start.12
  59.6 3.6 %collective-permute-start.5 = (f32[2,2,128,256]{3,2,1,0:T(8,128)S(1)}, f32[2,2,128,256]{3,2,1,0:T(8,128)S(1)}, u32[]{:S(2)}, u32[]{:S(2)}) collective-permute-start(f32[2,2,128,256]{3,2,1,0:T(8,128)S(1)} %maximum_select_fusion.1), channel_id=1, source_target_pairs={{0,1},{1,0},{2,3},{3,2},{4,5},{5,4},{6,7},{7,6},{8,9},{9,8},{10,11... | collective-permute-start | bytes 1572872 | tf_op jit(solution)/shard_map/ppermute | solution.py:168
  63.2 1.5 %collective-permute-done.5.args_8_ = f32[2,2,128,256]{3,2,1,0:T(8,128)S(1)} collective-permute-done((f32[2,2,128,256]{3,2,1,0:T(8,128)S(1)}, f32[2,2,128,256]{3,2,1,0:T(8,128)S(1)}, u32[]{:S(2)}, u32[]{:S(2)}) %collective-permute-start.5) | collective-permute-done | bytes 524320 | tf_op jit(solution)/shard_map/ppermute | solution.py:168
  64.7 1.7 %solve2.1.args_4_ = f32[2,128,256]{2,1,0:T(8,128)S(1)} custom-call(s32[8]{0:T(128)S(1)} %copy-done.7, s32[30]{0:T(128)S(1)} %copy-done.9, s32[30]{0:T(128)S(1)} %copy-done.11, f32[30,128,128]{2,1,0:T(8,128)S(1)} %copy-done.1, f32[8,128,128]{2,1,0:T(8,128)S(1)} %bitcast.14, f32[4,128,256]{2,1,0:T(8,128)S(1)} %get-tuple-element.22.args_5_, ...), custom_call_target="tpu_custom_call" | custom-call | tf_op jit(solution)/shard_map/solve2/pallas_call | solution.py:238
  66.4 1.9 %collective-permute-start.7 = (f32[2,128,256]{2,1,0:T(8,128)S(1)}, f32[2,128,256]{2,1,0:T(8,128)S(1)}, u32[]{:S(2)}, u32[]{:S(2)}) collective-permute-start(f32[2,128,256]{2,1,0:T(8,128)S(1)} %solve2.1.args_4_), channel_id=1, source_target_pairs={{0,4},{1,5},{2,6},{3,7},{4,8},{5,9},{6,10},{7,11},{8,12},{9,13},{1... | collective-permute-start | bytes 786440 | tf_op jit(solution)/shard_map/ppermute | solution.py:165
  68.4 1.9 %collective-permute-start.6 = (f32[2,128,256]{2,1,0:T(8,128)S(1)}, f32[2,128,256]{2,1,0:T(8,128)S(1)}, u32[]{:S(2)}, u32[]{:S(2)}) collective-permute-start(f32[2,128,256]{2,1,0:T(8,128)S(1)} %solve2.1.args_4_), channel_id=1, source_target_pairs={{0,2},{1,3},{2,4},{3,5},{4,6},{5,7},{6,8},{7,9},{8,10},{9,11},{10,... | collective-permute-start | bytes 786440 | tf_op jit(solution)/shard_map/ppermute | solution.py:165
  70.3 0.0 copy-done.8
  70.3 0.0 copy-done.10
  70.3 0.0 copy-done.12
  70.3 1.7 %window2.1 = (f32[8,128,256]{2,1,0:T(8,128)}, f32[2,128,256]{2,1,0:T(8,128)S(1)}) custom-call(s32[8]{0:T(128)S(1)} %copy-done.8, s32[30]{0:T(128)S(1)} %copy-done.10, s32[30]{0:T(128)S(1)} %copy-done.12, f32[30,128,128]{2,1,0:T(8,128)S(1)} %copy-done.1, f32[2,128,256]{2,1,0:T(8,128)S(1)} %solve2.1.args_4_, ...), custom_call_target="tpu_custom_call", output_to_operand_aliasing={{0}: (9, {})} | custom-call | flops 503316480 | bytes 3145728 | tf_op jit(solution)/shard_map/window2/pallas_call | solution.py:215
  72.0 13.0 %collective-permute-done.7.args_7_ = f32[2,128,256]{2,1,0:T(8,128)S(1)} collective-permute-done((f32[2,128,256]{2,1,0:T(8,128)S(1)}, f32[2,128,256]{2,1,0:T(8,128)S(1)}, u32[]{:S(2)}, u32[]{:S(2)}) %collective-permute-start.7) | collective-permute-done | bytes 262176 | tf_op jit(solution)/shard_map/ppermute | solution.py:165
  85.0 1.9 %collective-permute-done.6.args_6_ = f32[2,128,256]{2,1,0:T(8,128)S(1)} collective-permute-done((f32[2,128,256]{2,1,0:T(8,128)S(1)}, f32[2,128,256]{2,1,0:T(8,128)S(1)}, u32[]{:S(2)}, u32[]{:S(2)}) %collective-permute-start.6) | collective-permute-done | bytes 262176 | tf_op jit(solution)/shard_map/ppermute | solution.py:165
  86.9 0.1 maximum_select_fusion.2
  86.9 3.4 %collective-permute-start.8 = (f32[2,2,128,256]{3,2,1,0:T(8,128)S(1)}, f32[2,2,128,256]{3,2,1,0:T(8,128)S(1)}, u32[]{:S(2)}, u32[]{:S(2)}) collective-permute-start(f32[2,2,128,256]{3,2,1,0:T(8,128)S(1)} %maximum_select_fusion.2), channel_id=1, source_target_pairs={{0,1},{1,0},{2,3},{3,2},{4,5},{5,4},{6,7},{7,6},{8,9},{9,8},{10,11... | collective-permute-start | bytes 1572872 | tf_op jit(solution)/shard_map/ppermute | solution.py:168
  90.4 1.5 %collective-permute-done.8.args_8_ = f32[2,2,128,256]{3,2,1,0:T(8,128)S(1)} collective-permute-done((f32[2,2,128,256]{3,2,1,0:T(8,128)S(1)}, f32[2,2,128,256]{3,2,1,0:T(8,128)S(1)}, u32[]{:S(2)}, u32[]{:S(2)}) %collective-permute-start.8) | collective-permute-done | bytes 524320 | tf_op jit(solution)/shard_map/ppermute | solution.py:168
  91.9 2.4 %solve3.1 = f32[8,128,256]{2,1,0:T(8,128)} custom-call(s32[8]{0:T(128)S(1)} %copy-done.8, s32[30]{0:T(128)S(1)} %copy-done.10, s32[30]{0:T(128)S(1)} %copy-done.12, f32[30,128,128]{2,1,0:T(8,128)S(1)} %copy-done.1, f32[8,128,128]{2,1,0:T(8,128)S(1)} %bitcast.15, f32[2,128,256]{2,1,0:T(8,128)S(1)} %get-tuple-element.26.args_5_, ...), custom_call_target="tpu_custom_call", output_to_operand_aliasing={{}: (9, {})} | custom-call | tf_op jit(solution)/shard_map/solve3/pallas_call | solution.py:238
  (6 shorter events, 0.0 us)
Async XLA Ops:
  0.0 1.0 %copy-start.2 = (f32[1024,128]{1,0:T(8,128)S(1)}, f32[1024,128]{1,0:T(8,128)}, u32[]{:S(2)}) copy-start(f32[1024,128]{1,0:T(8,128)} %param.7) | copy-start | bytes 1572868
  1.0 1.2 %copy-start.4 = (f32[1024,256]{1,0:T(8,128)S(1)}, f32[1024,256]{1,0:T(8,128)}, u32[]{:S(2)}) copy-start(f32[1024,256]{1,0:T(8,128)} %param.6) | copy-start | bytes 3145732
  2.3 0.7 copy-start.6
  2.9 9.3 %copy-start.5 = (f32[1024,256]{1,0:T(8,128)S(1)}, f32[1024,256]{1,0:T(8,128)}, u32[]{:S(2)}) copy-start(f32[1024,256]{1,0:T(8,128)} %param.6) | copy-start | bytes 3145732
  4.3 22.8 %collective-permute-start.1 = (f32[2,128,256]{2,1,0:T(8,128)S(1)}, f32[2,128,256]{2,1,0:T(8,128)S(1)}, u32[]{:S(2)}, u32[]{:S(2)}) collective-permute-start(f32[2,128,256]{2,1,0:T(8,128)S(1)} %first.1.args_4_), channel_id=1, source_target_pairs={{0,4},{1,5},{2,6},{3,7},{4,8},{5,9},{6,10},{7,11},{8,12},{9,13},{1... | collective-permute-start | bytes 786440 | tf_op jit(solution)/shard_map/ppermute | solution.py:165
  9.9 22.6 %collective-permute-start = (f32[2,128,256]{2,1,0:T(8,128)S(1)}, f32[2,128,256]{2,1,0:T(8,128)S(1)}, u32[]{:S(2)}, u32[]{:S(2)}) collective-permute-start(f32[2,128,256]{2,1,0:T(8,128)S(1)} %first.1.args_4_), channel_id=1, source_target_pairs={{0,2},{1,3},{2,4},{3,5},{4,6},{5,7},{6,8},{7,9},{8,10},{9,11},{10,... | collective-permute-start | bytes 786440 | tf_op jit(solution)/shard_map/ppermute | solution.py:165
  12.2 1.5 %copy-start = (f32[30,128,128]{2,1,0:T(8,128)S(1)}, f32[30,128,128]{2,1,0:T(8,128)}, u32[]{:S(2)}) copy-start(f32[30,128,128]{2,1,0:T(8,128)} %args_3_.14) | copy-start | bytes 5898244
  13.8 0.7 copy-start.7
  14.4 0.7 copy-start.9
  15.1 0.7 copy-start.11
  15.8 21.6 %copy-start.1 = (f32[30,128,128]{2,1,0:T(8,128)S(1)}, f32[30,128,128]{2,1,0:T(8,128)}, u32[]{:S(2)}) copy-start(f32[30,128,128]{2,1,0:T(8,128)} %args_3_.14) | copy-start | bytes 5898244
  15.8 21.6 %copy-start.3 = (f32[1024,128]{1,0:T(8,128)S(1)}, f32[1024,128]{1,0:T(8,128)}, u32[]{:S(2)}) copy-start(f32[1024,128]{1,0:T(8,128)} %param.7) | copy-start | bytes 1572868
  32.5 4.9 %collective-permute-start.2 = (f32[2,2,128,256]{3,2,1,0:T(8,128)S(1)}, f32[2,2,128,256]{3,2,1,0:T(8,128)S(1)}, u32[]{:S(2)}, u32[]{:S(2)}) collective-permute-start(f32[2,2,128,256]{3,2,1,0:T(8,128)S(1)} %maximum_select_fusion), channel_id=1, source_target_pairs={{0,1},{1,0},{2,3},{3,2},{4,5},{5,4},{6,7},{7,6},{8,9},{9,8},{10,11... | collective-permute-start | bytes 1572872 | tf_op jit(solution)/shard_map/ppermute | solution.py:168
  39.1 18.6 %collective-permute-start.4 = (f32[2,128,256]{2,1,0:T(8,128)S(1)}, f32[2,128,256]{2,1,0:T(8,128)S(1)}, u32[]{:S(2)}, u32[]{:S(2)}) collective-permute-start(f32[2,128,256]{2,1,0:T(8,128)S(1)} %solve1.1.args_4_), channel_id=1, source_target_pairs={{0,4},{1,5},{2,6},{3,7},{4,8},{5,9},{6,10},{7,11},{8,12},{9,13},{1... | collective-permute-start | bytes 786440 | tf_op jit(solution)/shard_map/ppermute | solution.py:165
  41.0 18.5 %collective-permute-start.3 = (f32[2,128,256]{2,1,0:T(8,128)S(1)}, f32[2,128,256]{2,1,0:T(8,128)S(1)}, u32[]{:S(2)}, u32[]{:S(2)}) collective-permute-start(f32[2,128,256]{2,1,0:T(8,128)S(1)} %solve1.1.args_4_), channel_id=1, source_target_pairs={{0,2},{1,3},{2,4},{3,5},{4,6},{5,7},{6,8},{7,9},{8,10},{9,11},{10,... | collective-permute-start | bytes 786440 | tf_op jit(solution)/shard_map/ppermute | solution.py:165
  59.6 10.7 %copy-start.8 = (s32[8]{0:T(128)S(1)}, s32[8]{0:T(128)}, u32[]{:S(2)}) copy-start(s32[8]{0:T(128)} %args_0_.14) | copy-start | bytes 100
  59.6 10.7 %copy-start.10 = (s32[30]{0:T(128)S(1)}, s32[30]{0:T(128)}, u32[]{:S(2)}) copy-start(s32[30]{0:T(128)} %args_1_.14) | copy-start | bytes 364
  59.6 10.7 %copy-start.12 = (s32[30]{0:T(128)S(1)}, s32[30]{0:T(128)}, u32[]{:S(2)}) copy-start(s32[30]{0:T(128)} %args_2_.14) | copy-start | bytes 364
  59.6 5.1 %collective-permute-start.5 = (f32[2,2,128,256]{3,2,1,0:T(8,128)S(1)}, f32[2,2,128,256]{3,2,1,0:T(8,128)S(1)}, u32[]{:S(2)}, u32[]{:S(2)}) collective-permute-start(f32[2,2,128,256]{3,2,1,0:T(8,128)S(1)} %maximum_select_fusion.1), channel_id=1, source_target_pairs={{0,1},{1,0},{2,3},{3,2},{4,5},{5,4},{6,7},{7,6},{8,9},{9,8},{10,11... | collective-permute-start | bytes 1572872 | tf_op jit(solution)/shard_map/ppermute | solution.py:168
  66.4 18.6 %collective-permute-start.7 = (f32[2,128,256]{2,1,0:T(8,128)S(1)}, f32[2,128,256]{2,1,0:T(8,128)S(1)}, u32[]{:S(2)}, u32[]{:S(2)}) collective-permute-start(f32[2,128,256]{2,1,0:T(8,128)S(1)} %solve2.1.args_4_), channel_id=1, source_target_pairs={{0,4},{1,5},{2,6},{3,7},{4,8},{5,9},{6,10},{7,11},{8,12},{9,13},{1... | collective-permute-start | bytes 786440 | tf_op jit(solution)/shard_map/ppermute | solution.py:165
  68.4 18.5 %collective-permute-start.6 = (f32[2,128,256]{2,1,0:T(8,128)S(1)}, f32[2,128,256]{2,1,0:T(8,128)S(1)}, u32[]{:S(2)}, u32[]{:S(2)}) collective-permute-start(f32[2,128,256]{2,1,0:T(8,128)S(1)} %solve2.1.args_4_), channel_id=1, source_target_pairs={{0,2},{1,3},{2,4},{3,5},{4,6},{5,7},{6,8},{7,9},{8,10},{9,11},{10,... | collective-permute-start | bytes 786440 | tf_op jit(solution)/shard_map/ppermute | solution.py:165
  86.9 5.0 %collective-permute-start.8 = (f32[2,2,128,256]{3,2,1,0:T(8,128)S(1)}, f32[2,2,128,256]{3,2,1,0:T(8,128)S(1)}, u32[]{:S(2)}, u32[]{:S(2)}) collective-permute-start(f32[2,2,128,256]{3,2,1,0:T(8,128)S(1)} %maximum_select_fusion.2), channel_id=1, source_target_pairs={{0,1},{1,0},{2,3},{3,2},{4,5},{5,4},{6,7},{7,6},{8,9},{9,8},{10,11... | collective-permute-start | bytes 1572872 | tf_op jit(solution)/shard_map/ppermute | solution.py:168
